TPU v7x, 32 devices: a whole 2x2x4 slice. The times are simulated.
32 devices in a mesh: dp: 4 (over y, x), row: 2 (over core), col: 4 (over z).
Axes of the slice: x: 2, y: 2, z: 4, core: 2. Of those that a mesh axis runs over, the one named last changes fastest.
Arguments:
- hidden_in: bfloat16 [8192, 768], P(('dp', 'col'), 'row'), may hold values from -36 to 36
- enc_states: bfloat16 [2048, 768], P(('dp', 'col'), 'row'), may hold values from -8 to 8
- grad_out: bfloat16 [8192, 768], P(('dp', 'col'), 'row'), may hold values from -6 to 6
- lengths: int32 [4], P('dp'), may hold values from 1024 to 2048, as said below
- buckets: int32 [2048], replicated, may hold values from 0 to 31, as said below
- self_gain: float32 [768], P('row'), may hold values from 0.1 to 1.9
- q_self: bfloat16 [768, 768], P('col', 'row'), may hold values from -0.02734375 to 0.02734375
- k_self: bfloat16 [768, 768], P('col', 'row'), may hold values from -0.21875 to 0.21875
- v_self: bfloat16 [768, 768], P('col', 'row'), may hold values from -0.21875 to 0.21875
- o_self: bfloat16 [768, 768], P('row', 'col'), may hold values from -2.5 to 2.5
- rel_table: float32 [12, 32], P('row'), may hold values from -4 to 4
- cross_gain: float32 [768], P('row'), may hold values from 0.1 to 1.9
- q_cross: bfloat16 [768, 768], P('col', 'row'), may hold values from -0.02734375 to 0.02734375
- k_cross: bfloat16 [768, 768], P('col', 'row'), may hold values from -0.21875 to 0.21875
- v_cross: bfloat16 [768, 768], P('col', 'row'), may hold values from -0.21875 to 0.21875
- o_cross: bfloat16 [768, 768], P('row', 'col'), may hold values from -2.5 to 2.5
- ff_gain: float32 [768], P('row'), may hold values from 0.1 to 1.9
- ff_gate: bfloat16 [768, 2048], P('col', 'row'), may hold values from -0.21875 to 0.21875
- ff_up: bfloat16 [768, 2048], P('col', 'row'), may hold values from -0.21875 to 0.21875
- ff_out: bfloat16 [2048, 768], P('row', 'col'), may hold values from -0.125 to 0.125
Outputs:
- out: bfloat16 [8192, 768], P(('dp', 'col'), 'row')
- grad_in: float32 [8192, 768], P(('dp', 'col'), 'row')
- grad_enc: float32 [2048, 768], P(('dp', 'col'), 'row')
- grad_self_gain: float32 [768], P('row')
- grad_q_self: float32 [768, 768], P('col', 'row')
- grad_k_self: float32 [768, 768], P('col', 'row')
- grad_v_self: float32 [768, 768], P('col', 'row')
- grad_o_self: float32 [768, 768], P('row', 'col')
- grad_rel_table: float32 [12, 32], P('row')
- grad_cross_gain: float32 [768], P('row')
- grad_q_cross: float32 [768, 768], P('col', 'row')
- grad_k_cross: float32 [768, 768], P('col', 'row')
- grad_v_cross: float32 [768, 768], P('col', 'row')
- grad_o_cross: float32 [768, 768], P('row', 'col')
- grad_ff_gain: float32 [768], P('row')
- grad_ff_gate: float32 [768, 2048], P('col', 'row')
- grad_ff_up: float32 [768, 2048], P('col', 'row')
- grad_ff_out: float32 [2048, 768], P('row', 'col')
Inputs may be any that keep to these rules, and one draw needn't show every extreme that they name: `lengths`: some sequence has exactly 2048 valid tokens. Distance d has bucket d for d < 16; buckets never fall as the distance grows; distance 2048 - 1 has bucket 32 - 1.
All inputs are finite; a program needn't handle non-finite values.
Results may differ from a plain program's by a relative error of at most 0.025.
Values may be sent and summed in bfloat16 or wider, within the bound.
No kernel may reach another device: no remote copies, remote signals or barrier semaphores. Data moves between devices by JAX's collectives and lax.ppermute only.
A program may use at most 320 MiB of HBM per device.

v0:
```python
from functools import partial

import jax
import jax.numpy as jnp
from jax import lax
from jax.sharding import PartitionSpec as P

D = 768
HS = 64


EPSILON = 1e-06
NEGATIVE = -1e30
GELU_SCALE = 0.7978845608028654


def matmul(left_side, right_side):
    return jnp.dot(left_side, right_side, preferred_element_type=jnp.float32)


def matmul_t(left_side, right_side):
    return lax.dot_general(
        left_side, right_side, (((1,), (1,)), ((), ())), preferred_element_type=jnp.float32
    )


def tokens_t(left_side, right_side):
    return lax.dot_general(
        left_side, right_side, (((0,), (0,)), ((), ())), preferred_element_type=jnp.float32
    )


def gelu_parts(gate_in):
    inner_arg = GELU_SCALE * (gate_in + 0.044715 * gate_in * gate_in * gate_in)
    tangent = jnp.tanh(inner_arg)
    gelu_value = 0.5 * gate_in * (1.0 + tangent)
    gelu_slope = 0.5 * (1.0 + tangent) + 0.5 * gate_in * (1.0 - tangent * tangent) * GELU_SCALE * (
        1.0 + 3.0 * 0.044715 * gate_in * gate_in
    )
    return (gelu_value, gelu_slope)


def row_stats(values):
    return lax.psum(values, "row")


def norm_forward(hidden, gain_vec):
    totals = row_stats(jnp.sum(hidden * hidden, axis=1))
    scales = lax.rsqrt(totals / D + EPSILON)[:, None]
    normed = hidden * scales
    return (normed, scales, (normed * gain_vec).astype(jnp.bfloat16))


def norm_backward(upstream, normed, scales, gain_vec):
    scaled_grad = upstream * gain_vec
    totals = row_stats(jnp.sum(scaled_grad * normed, axis=1))
    return (
        scales * (scaled_grad - normed * (totals / D)[:, None]),
        jnp.sum(upstream * normed, axis=0),
    )


def gather_feats(values):
    return lax.all_gather(values, "row", axis=1, tiled=True)


def sum_feats(values):
    return lax.psum_scatter(values, "row", scatter_dimension=1, tiled=True)


def sum_key_grads(grad_keys, grad_values):
    return (
        lax.psum_scatter(
            grad_keys.astype(jnp.bfloat16), "col", scatter_dimension=0, tiled=True
        ).astype(jnp.float32),
        lax.psum_scatter(
            grad_values.astype(jnp.bfloat16), "col", scatter_dimension=0, tiled=True
        ).astype(jnp.float32),
    )


def toeplitz(bias_dist, first_row, row_total):
    head_count, seq_len = bias_dist.shape
    span_width = seq_len + row_total
    column = jnp.arange(span_width)
    distance = jnp.where(column < seq_len, first_row - column, first_row + span_width - column)
    inside = (distance >= 0) & (distance < seq_len)
    picked = jnp.take(bias_dist, jnp.clip(distance, 0, seq_len - 1), axis=1)
    ramp_row = jnp.where(inside[None, :], picked, 0.0)
    tiled_rows = jnp.broadcast_to(
        ramp_row[:, None, :], (head_count, row_total, span_width)
    ).reshape(head_count, row_total * span_width)
    shifted = tiled_rows[:, : row_total * (span_width - 1)].reshape(
        head_count, row_total, span_width - 1
    )
    return shifted[:, :, :seq_len]


def head_view(values):
    return values.reshape(values.shape[0], values.shape[1] // HS, HS)


def raw_scores(queries, key_mat, bias_block, allowed):
    scores = jnp.einsum(
        "qhd,khd->hqk", head_view(queries), head_view(key_mat), preferred_element_type=jnp.float32
    )
    if bias_block is not None:
        scores = scores + bias_block
    if allowed is not None:
        scores = jnp.where(allowed[None], scores, NEGATIVE)
    return scores


def attend_forward(queries, key_mat, value_mat, bias_block, allowed):
    scores = raw_scores(queries, key_mat, bias_block, allowed)
    row_peak = jnp.max(scores, axis=2, keepdims=True)
    log_total = row_peak + jnp.log(jnp.sum(jnp.exp(scores - row_peak), axis=2, keepdims=True))
    prob_block = jnp.exp(scores - log_total).astype(jnp.bfloat16)
    context = jnp.einsum(
        "hqk,khd->qhd", prob_block, head_view(value_mat), preferred_element_type=jnp.float32
    )
    return (context.reshape(queries.shape[0], queries.shape[1]).astype(jnp.bfloat16), log_total)


def attend_backward(
    queries, key_mat, value_mat, bias_block, allowed, log_total, context, grad_context
):
    scores = raw_scores(queries, key_mat, bias_block, allowed)
    prob_full = jnp.exp(scores - log_total)
    grad_heads = head_view(grad_context)
    grad_prob = jnp.einsum(
        "qhd,khd->hqk", grad_heads, head_view(value_mat), preferred_element_type=jnp.float32
    )
    row_delta = jnp.einsum(
        "qhd,qhd->hq", grad_heads.astype(jnp.float32), head_view(context).astype(jnp.float32)
    )
    dscore = prob_full * (grad_prob - row_delta[:, :, None])
    prob_block = prob_full.astype(jnp.bfloat16)
    dscore_b = dscore.astype(jnp.bfloat16)
    width_all = queries.shape[1]
    key_count = key_mat.shape[0]
    grad_values = jnp.einsum(
        "hqk,qhd->khd", prob_block, grad_heads, preferred_element_type=jnp.float32
    ).reshape(key_count, width_all)
    grad_keys = jnp.einsum(
        "hqk,qhd->khd", dscore_b, head_view(queries), preferred_element_type=jnp.float32
    ).reshape(key_count, width_all)
    grad_query = jnp.einsum(
        "hqk,khd->qhd", dscore_b, head_view(key_mat), preferred_element_type=jnp.float32
    ).reshape(queries.shape[0], width_all)
    return (grad_query, grad_keys, grad_values, dscore)


def per_device(
    hidden_in,
    enc_states,
    grad_out,
    lengths,
    buckets,
    self_gain,
    q_self,
    k_self,
    v_self,
    o_self,
    rel_table,
    cross_gain,
    q_cross,
    k_cross,
    v_cross,
    o_cross,
    ff_gain,
    ff_gate,
    ff_up,
    ff_out,
):
    local_rows = hidden_in.shape[0]
    seq_len = local_rows * lax.axis_size("col")
    first_query = lax.axis_index("col") * local_rows
    head_cols = q_self.shape[1]
    ff_cols = ff_gate.shape[1]
    positions = jnp.arange(seq_len)
    valid_length = lengths[0]
    bucket_onehot = (buckets[:, None] == jnp.arange(rel_table.shape[1])[None, :]).astype(
        jnp.float32
    )
    bias_dist = jnp.dot(rel_table, bucket_onehot.T, precision=lax.Precision.HIGHEST)
    bias_block, bias_pull = jax.vjp(
        partial(toeplitz, first_row=first_query, row_total=local_rows), bias_dist
    )
    query_pos = first_query + jnp.arange(local_rows)
    allowed = (positions[None, :] <= query_pos[:, None]) & (positions[None, :] < valid_length)
    full = (
        lax.all_gather(q_self, "col", axis=0, tiled=True),
        lax.all_gather(k_self, "col", axis=0, tiled=True),
        lax.all_gather(v_self, "col", axis=0, tiled=True),
        lax.all_gather(o_self, "col", axis=1, tiled=True),
        lax.all_gather(q_cross, "col", axis=0, tiled=True),
        lax.all_gather(k_cross, "col", axis=0, tiled=True),
        lax.all_gather(v_cross, "col", axis=0, tiled=True),
        lax.all_gather(o_cross, "col", axis=1, tiled=True),
        lax.all_gather(ff_gate, "col", axis=0, tiled=True),
        lax.all_gather(ff_up, "col", axis=0, tiled=True),
        lax.all_gather(ff_out, "col", axis=1, tiled=True),
    )
    w_qkv = jnp.concatenate([full[0], full[1], full[2]], axis=1)
    w_ckv = jnp.concatenate([full[5], full[6]], axis=1)
    w_ff = jnp.concatenate([full[8], full[9]], axis=1)
    residual = hidden_in.astype(jnp.float32)
    normed1, scales1, input1 = norm_forward(residual, self_gain)
    whole1 = gather_feats(input1)
    enc_whole = gather_feats(enc_states)
    qkv = matmul(whole1, w_qkv).astype(jnp.bfloat16)
    self_queries = qkv[:, :head_cols]
    cross_own = matmul(enc_whole, w_ckv).astype(jnp.bfloat16)
    self_keys, self_values, cross_keys, cross_values = (
        lax.all_gather(qkv[:, head_cols : 2 * head_cols], "col", axis=0, tiled=True),
        lax.all_gather(qkv[:, 2 * head_cols :], "col", axis=0, tiled=True),
        lax.all_gather(cross_own[:, :head_cols], "col", axis=0, tiled=True),
        lax.all_gather(cross_own[:, head_cols:], "col", axis=0, tiled=True),
    )
    context, log_sums = attend_forward(self_queries, self_keys, self_values, bias_block, allowed)
    after_self = residual + sum_feats(matmul(context, full[3]))
    normed2, scales2, input2 = norm_forward(after_self, cross_gain)
    whole2 = gather_feats(input2)
    cross_q = matmul(whole2, full[4]).astype(jnp.bfloat16)
    cross_ctx, cross_sums = attend_forward(cross_q, cross_keys, cross_values, None, None)
    after_cross = after_self + sum_feats(matmul(cross_ctx, full[7]))
    normed3, scales3, input3 = norm_forward(after_cross, ff_gain)
    whole3 = gather_feats(input3)
    gate_up = matmul(whole3, w_ff)
    gate_part = gate_up[:, :ff_cols]
    up_part = gate_up[:, ff_cols:]
    activated, gelu_slope = gelu_parts(gate_part)
    hidden_units = (activated * up_part).astype(jnp.bfloat16)
    output = (after_cross + sum_feats(matmul(hidden_units, full[10]))).astype(jnp.bfloat16)
    again = (
        lax.all_gather(q_self, "col", axis=0, tiled=True),
        lax.all_gather(k_self, "col", axis=0, tiled=True),
        lax.all_gather(v_self, "col", axis=0, tiled=True),
        lax.all_gather(o_self, "col", axis=1, tiled=True),
        lax.all_gather(q_cross, "col", axis=0, tiled=True),
        lax.all_gather(k_cross, "col", axis=0, tiled=True),
        lax.all_gather(v_cross, "col", axis=0, tiled=True),
        lax.all_gather(o_cross, "col", axis=1, tiled=True),
        lax.all_gather(ff_gate, "col", axis=0, tiled=True),
        lax.all_gather(ff_up, "col", axis=0, tiled=True),
        lax.all_gather(ff_out, "col", axis=1, tiled=True),
    )
    back_qkv = jnp.concatenate([again[0], again[1], again[2]], axis=1)
    back_ckv = jnp.concatenate([again[5], again[6]], axis=1)
    back_ff = jnp.concatenate([again[8], again[9]], axis=1)
    upstream = grad_out.astype(jnp.float32)
    upstream_all = gather_feats(grad_out)
    grad_hidden = matmul_t(upstream_all, again[10])
    grad_ff_out = tokens_t(hidden_units, upstream_all)
    grad_gate_up = jnp.concatenate(
        [grad_hidden * up_part * gelu_slope, grad_hidden * activated], axis=1
    ).astype(jnp.bfloat16)
    grad_input3 = sum_feats(matmul_t(grad_gate_up, back_ff))
    grad_w_ff = tokens_t(whole3, grad_gate_up)
    grad_part3, grad_ff_gain = norm_backward(grad_input3, normed3, scales3, ff_gain)
    grad_after_cross = upstream + grad_part3
    down_cross_all = gather_feats(grad_after_cross.astype(jnp.bfloat16))
    grad_o_cross = tokens_t(cross_ctx, down_cross_all)
    grad_cross_ctx = matmul_t(down_cross_all, again[7]).astype(jnp.bfloat16)
    grad_cq, grad_ck, grad_cv, unused_cross = attend_backward(
        cross_q, cross_keys, cross_values, None, None, cross_sums, cross_ctx, grad_cross_ctx
    )
    summed_ck, summed_cv = sum_key_grads(grad_ck, grad_cv)
    grad_ckv = jnp.concatenate([summed_ck, summed_cv], axis=1).astype(jnp.bfloat16)
    grad_cq_b = grad_cq.astype(jnp.bfloat16)
    grad_q_cross = tokens_t(whole2, grad_cq_b)
    grad_w_ckv = tokens_t(enc_whole, grad_ckv)
    grad_encoder = sum_feats(matmul_t(grad_ckv, back_ckv))
    grad_input2 = sum_feats(matmul_t(grad_cq_b, again[4]))
    grad_part2, grad_cross_gain = norm_backward(grad_input2, normed2, scales2, cross_gain)
    grad_after_self = grad_after_cross + grad_part2
    down_self_all = gather_feats(grad_after_self.astype(jnp.bfloat16))
    grad_o_self = tokens_t(context, down_self_all)
    grad_context = matmul_t(down_self_all, again[3]).astype(jnp.bfloat16)
    grad_q, grad_k, grad_v, dscore = attend_backward(
        self_queries, self_keys, self_values, bias_block, allowed, log_sums, context, grad_context
    )
    grad_dist = bias_pull(dscore)[0]
    grad_table = jnp.dot(grad_dist, bucket_onehot, precision=lax.Precision.HIGHEST)
    summed_k, summed_v = sum_key_grads(grad_k, grad_v)
    grad_qkv = jnp.concatenate([grad_q, summed_k, summed_v], axis=1).astype(jnp.bfloat16)
    grad_w_qkv = tokens_t(whole1, grad_qkv)
    grad_input1 = sum_feats(matmul_t(grad_qkv, back_qkv))
    grad_part1, grad_self_gain = norm_backward(grad_input1, normed1, scales1, self_gain)
    grad_input = grad_after_self + grad_part1
    reduced = (
        lax.psum_scatter(
            grad_w_qkv[:, :head_cols].astype(jnp.bfloat16), "col", scatter_dimension=0, tiled=True
        ).astype(jnp.float32),
        lax.psum_scatter(
            grad_w_qkv[:, head_cols : 2 * head_cols].astype(jnp.bfloat16),
            "col",
            scatter_dimension=0,
            tiled=True,
        ).astype(jnp.float32),
        lax.psum_scatter(
            grad_w_qkv[:, 2 * head_cols :].astype(jnp.bfloat16),
            "col",
            scatter_dimension=0,
            tiled=True,
        ).astype(jnp.float32),
        lax.psum_scatter(
            grad_o_self.astype(jnp.bfloat16), "col", scatter_dimension=1, tiled=True
        ).astype(jnp.float32),
        lax.psum_scatter(
            grad_q_cross.astype(jnp.bfloat16), "col", scatter_dimension=0, tiled=True
        ).astype(jnp.float32),
        lax.psum_scatter(
            grad_w_ckv[:, :head_cols].astype(jnp.bfloat16), "col", scatter_dimension=0, tiled=True
        ).astype(jnp.float32),
        lax.psum_scatter(
            grad_w_ckv[:, head_cols:].astype(jnp.bfloat16), "col", scatter_dimension=0, tiled=True
        ).astype(jnp.float32),
        lax.psum_scatter(
            grad_o_cross.astype(jnp.bfloat16), "col", scatter_dimension=1, tiled=True
        ).astype(jnp.float32),
        lax.psum_scatter(
            grad_w_ff[:, :ff_cols].astype(jnp.bfloat16), "col", scatter_dimension=0, tiled=True
        ).astype(jnp.float32),
        lax.psum_scatter(
            grad_w_ff[:, ff_cols:].astype(jnp.bfloat16), "col", scatter_dimension=0, tiled=True
        ).astype(jnp.float32),
        lax.psum_scatter(
            grad_ff_out.astype(jnp.bfloat16), "col", scatter_dimension=1, tiled=True
        ).astype(jnp.float32),
    )
    summed = (
        lax.psum(reduced[0].astype(jnp.bfloat16), "dp").astype(jnp.float32),
        lax.psum(reduced[1].astype(jnp.bfloat16), "dp").astype(jnp.float32),
        lax.psum(reduced[2].astype(jnp.bfloat16), "dp").astype(jnp.float32),
        lax.psum(reduced[3].astype(jnp.bfloat16), "dp").astype(jnp.float32),
        lax.psum(reduced[4].astype(jnp.bfloat16), "dp").astype(jnp.float32),
        lax.psum(reduced[5].astype(jnp.bfloat16), "dp").astype(jnp.float32),
        lax.psum(reduced[6].astype(jnp.bfloat16), "dp").astype(jnp.float32),
        lax.psum(reduced[7].astype(jnp.bfloat16), "dp").astype(jnp.float32),
        lax.psum(reduced[8].astype(jnp.bfloat16), "dp").astype(jnp.float32),
        lax.psum(reduced[9].astype(jnp.bfloat16), "dp").astype(jnp.float32),
        lax.psum(reduced[10].astype(jnp.bfloat16), "dp").astype(jnp.float32),
    )
    small = lax.psum((grad_self_gain, grad_cross_gain, grad_ff_gain, grad_table), ("dp", "col"))
    return (
        output,
        grad_input,
        grad_encoder,
        small[0],
        summed[0],
        summed[1],
        summed[2],
        summed[3],
        small[3],
        small[1],
        summed[4],
        summed[5],
        summed[6],
        summed[7],
        small[2],
        summed[8],
        summed[9],
        summed[10],
    )


def solution(mesh):
    return jax.shard_map(
        per_device,
        mesh=mesh,
        in_specs=(
            P(("dp", "col"), "row"),
            P(("dp", "col"), "row"),
            P(("dp", "col"), "row"),
            P("dp"),
            P(),
            P("row"),
            P("col", "row"),
            P("col", "row"),
            P("col", "row"),
            P("row", "col"),
            P("row", None),
            P("row"),
            P("col", "row"),
            P("col", "row"),
            P("col", "row"),
            P("row", "col"),
            P("row"),
            P("col", "row"),
            P("col", "row"),
            P("row", "col"),
        ),
        out_specs=(
            P(("dp", "col"), "row"),
            P(("dp", "col"), "row"),
            P(("dp", "col"), "row"),
            P("row"),
            P("col", "row"),
            P("col", "row"),
            P("col", "row"),
            P("row", "col"),
            P("row", None),
            P("row"),
            P("col", "row"),
            P("col", "row"),
            P("col", "row"),
            P("row", "col"),
            P("row"),
            P("col", "row"),
            P("col", "row"),
            P("row", "col"),
        ),
        check_vma=False,
    )
```

profile of v0, /device:TPU:0, one launch (start us, length us, event | category | flops | bytes accessed | tf_op | source)
XLA Modules:
  0.0 2404.9 jit_solution(318419249263386690)
XLA Ops:
  101.7 52.3 %copy.105 = f32[1,6,512,2560]{3,1,2,0:T(8,128)} copy(f32[1,6,512,2560]{3,2,1,0:T(8,128)S(1)} %broadcast_bitcast_fusion) | data formatting | bytes 62914560
  182.0 599.7 %while.2 = (u32[]{:T(128)}, f32[1,6,1310208]{2,1,0:T(8,128)}, f32[7861248]{0:T(1024)}, u32[]{}, f32[]{:T(128)}, /*index=5*/u32[]{}, u32[]{}, u32[]{}) while((u32[]{:T(128)}, f32[1,6,1310208]{2,1,0:T(8,128)}, f32[7861248]{0:T(1024)}, u32[]{}, f32[]{:T(128)}, /*index=5*/u32[]{}, u32[]{}, u32[]{}) %tuple.55), condition=%wide.cond, body=%wide.body.sunk | while | flops 9 | bytes 20963528
  182.6 54.1 %dynamic-slice_reduce_fusion.2 = f32[1310208]{0:T(1024)} fusion(f32[]{:T(128)} %broadcast.240, f32[1,6,1310208]{2,1,0:T(8,128)} %get-tuple-element.198, u32[]{:T(128)S(6)} %multiply.30, u32[]{:T(128)S(6)} %multiply.31), kind=kLoop, calls=%fused_computation.146.clone.1 | loop fusion | bytes 10481676
  236.7 45.5 %dynamic-update-slice.18 = f32[7861248]{0:T(1024)} dynamic-update-slice(f32[7861248]{0:T(1024)} %get-tuple-element.191, f32[1310208]{0:T(1024)} %dynamic-slice_reduce_fusion.2, u32[]{:T(128)S(6)} %add.284) | dynamic-update-slice | bytes 10481668
  282.7 54.1 %dynamic-slice_reduce_fusion.2 = f32[1310208]{0:T(1024)} fusion(f32[]{:T(128)} %broadcast.240, f32[1,6,1310208]{2,1,0:T(8,128)} %get-tuple-element.198, u32[]{:T(128)S(6)} %multiply.30, u32[]{:T(128)S(6)} %multiply.31), kind=kLoop, calls=%fused_computation.146.clone.1 | loop fusion | bytes 10481676
  336.8 45.4 %dynamic-update-slice.18 = f32[7861248]{0:T(1024)} dynamic-update-slice(f32[7861248]{0:T(1024)} %get-tuple-element.191, f32[1310208]{0:T(1024)} %dynamic-slice_reduce_fusion.2, u32[]{:T(128)S(6)} %add.284) | dynamic-update-slice | bytes 10481668
  382.7 54.1 %dynamic-slice_reduce_fusion.2 = f32[1310208]{0:T(1024)} fusion(f32[]{:T(128)} %broadcast.240, f32[1,6,1310208]{2,1,0:T(8,128)} %get-tuple-element.198, u32[]{:T(128)S(6)} %multiply.30, u32[]{:T(128)S(6)} %multiply.31), kind=kLoop, calls=%fused_computation.146.clone.1 | loop fusion | bytes 10481676
  436.8 45.4 %dynamic-update-slice.18 = f32[7861248]{0:T(1024)} dynamic-update-slice(f32[7861248]{0:T(1024)} %get-tuple-element.191, f32[1310208]{0:T(1024)} %dynamic-slice_reduce_fusion.2, u32[]{:T(128)S(6)} %add.284) | dynamic-update-slice | bytes 10481668
  482.7 54.1 %dynamic-slice_reduce_fusion.2 = f32[1310208]{0:T(1024)} fusion(f32[]{:T(128)} %broadcast.240, f32[1,6,1310208]{2,1,0:T(8,128)} %get-tuple-element.198, u32[]{:T(128)S(6)} %multiply.30, u32[]{:T(128)S(6)} %multiply.31), kind=kLoop, calls=%fused_computation.146.clone.1 | loop fusion | bytes 10481676
  536.8 45.4 %dynamic-update-slice.18 = f32[7861248]{0:T(1024)} dynamic-update-slice(f32[7861248]{0:T(1024)} %get-tuple-element.191, f32[1310208]{0:T(1024)} %dynamic-slice_reduce_fusion.2, u32[]{:T(128)S(6)} %add.284) | dynamic-update-slice | bytes 10481668
  582.7 54.1 %dynamic-slice_reduce_fusion.2 = f32[1310208]{0:T(1024)} fusion(f32[]{:T(128)} %broadcast.240, f32[1,6,1310208]{2,1,0:T(8,128)} %get-tuple-element.198, u32[]{:T(128)S(6)} %multiply.30, u32[]{:T(128)S(6)} %multiply.31), kind=kLoop, calls=%fused_computation.146.clone.1 | loop fusion | bytes 10481676
  636.7 45.5 %dynamic-update-slice.18 = f32[7861248]{0:T(1024)} dynamic-update-slice(f32[7861248]{0:T(1024)} %get-tuple-element.191, f32[1310208]{0:T(1024)} %dynamic-slice_reduce_fusion.2, u32[]{:T(128)S(6)} %add.284) | dynamic-update-slice | bytes 10481668
  682.7 54.1 %dynamic-slice_reduce_fusion.2 = f32[1310208]{0:T(1024)} fusion(f32[]{:T(128)} %broadcast.240, f32[1,6,1310208]{2,1,0:T(8,128)} %get-tuple-element.198, u32[]{:T(128)S(6)} %multiply.30, u32[]{:T(128)S(6)} %multiply.31), kind=kLoop, calls=%fused_computation.146.clone.1 | loop fusion | bytes 10481676
  736.8 44.9 %dynamic-update-slice.18 = f32[7861248]{0:T(1024)} dynamic-update-slice(f32[7861248]{0:T(1024)} %get-tuple-element.191, f32[1310208]{0:T(1024)} %dynamic-slice_reduce_fusion.2, u32[]{:T(128)S(6)} %add.284) | dynamic-update-slice | bytes 10481668
  781.7 44.5 %reshape.256 = f32[6,512,2559]{2,1,0:T(8,128)} reshape(f32[7861248]{0:T(1024)} %get-tuple-element.76) | data formatting | bytes 62889984 | tf_op jit(solution)/shard_map/jvp()/reshape | solution.py:93
  1547.6 45.2 %reshape.300 = f32[7861248]{0:T(1024)} reshape(f32[6,512,2559]{2,1,0:T(8,128)} %pad.6) | data formatting | bytes 62889984
  1592.7 646.2 %while.3 = (u32[]{:T(128)}, f32[7861248]{0:T(1024)}, f32[1,6,1310208]{2,1,0:T(8,128)}, u32[]{}, u32[]{}, /*index=5*/u32[]{}, u32[]{}, u32[]{}) while((u32[]{:T(128)}, f32[7861248]{0:T(1024)}, f32[1,6,1310208]{2,1,0:T(8,128)}, u32[]{}, u32[]{}, /*index=5*/u32[]{}, u32[]{}, u32[]{}) %tuple.58), condition=%wide.cond.1, body=%wide.body.1.sunk | while | flops 9 | bytes 31445176
  1601.9 97.9 %dynamic-update-slice.19 = f32[1,6,1310208]{2,1,0:T(8,128)} dynamic-update-slice(f32[1,6,1310208]{2,1,0:T(8,128)} %get-tuple-element.215, f32[1,1,1310208]{2,1,0:T(1,128)} %reshape.303, u32[]{:T(128)S(6)} %multiply.34, u32[]{:T(128)S(6)} %multiply.36, u32[]{} %constant.214..sunk) | dynamic-update-slice | bytes 10481668
  1709.0 98.6 %dynamic-update-slice.19 = f32[1,6,1310208]{2,1,0:T(8,128)} dynamic-update-slice(f32[1,6,1310208]{2,1,0:T(8,128)} %get-tuple-element.215, f32[1,1,1310208]{2,1,0:T(1,128)} %reshape.303, u32[]{:T(128)S(6)} %multiply.34, u32[]{:T(128)S(6)} %multiply.36, u32[]{} %constant.214..sunk) | dynamic-update-slice | bytes 10481668
  1816.8 98.6 %dynamic-update-slice.19 = f32[1,6,1310208]{2,1,0:T(8,128)} dynamic-update-slice(f32[1,6,1310208]{2,1,0:T(8,128)} %get-tuple-element.215, f32[1,1,1310208]{2,1,0:T(1,128)} %reshape.303, u32[]{:T(128)S(6)} %multiply.34, u32[]{:T(128)S(6)} %multiply.36, u32[]{} %constant.214..sunk) | dynamic-update-slice | bytes 10481668
  1924.7 98.6 %dynamic-update-slice.19 = f32[1,6,1310208]{2,1,0:T(8,128)} dynamic-update-slice(f32[1,6,1310208]{2,1,0:T(8,128)} %get-tuple-element.215, f32[1,1,1310208]{2,1,0:T(1,128)} %reshape.303, u32[]{:T(128)S(6)} %multiply.34, u32[]{:T(128)S(6)} %multiply.36, u32[]{} %constant.214..sunk) | dynamic-update-slice | bytes 10481668
  2032.5 98.6 %dynamic-update-slice.19 = f32[1,6,1310208]{2,1,0:T(8,128)} dynamic-update-slice(f32[1,6,1310208]{2,1,0:T(8,128)} %get-tuple-element.215, f32[1,1,1310208]{2,1,0:T(1,128)} %reshape.303, u32[]{:T(128)S(6)} %multiply.34, u32[]{:T(128)S(6)} %multiply.36, u32[]{} %constant.214..sunk) | dynamic-update-slice | bytes 10481668
  2140.3 98.6 %dynamic-update-slice.19 = f32[1,6,1310208]{2,1,0:T(8,128)} dynamic-update-slice(f32[1,6,1310208]{2,1,0:T(8,128)} %get-tuple-element.215, f32[1,1,1310208]{2,1,0:T(1,128)} %reshape.303, u32[]{:T(128)S(6)} %multiply.34, u32[]{:T(128)S(6)} %multiply.36, u32[]{} %constant.214..sunk) | dynamic-update-slice | bytes 10481668
  2306.5 72.8 %all-reduce.2 = (f32[384]{0:T(512)}, f32[6,32]{1,0:T(8,128)}, f32[384]{0:T(512)}, f32[384]{0:T(512)}) all-reduce(f32[384]{0:T(512)S(1)} %get-tuple-element.86, f32[6,32]{1,0:T(8,128)S(1)} %fusion.38, f32[384]{0:T(512)} %get-tuple-element.84, f32[384]{0:T(512)} %get-tuple-element.82), channel_id=1, replica_groups=mesh['dp'=4,'row'=2,'col'=4] {'dp','col'}, use_global_device_ids=true, to_apply=%region_28.29 | all-reduce | flops 1344 | bytes 10752 | tf_op jit(solution)/shard_map/psum | solution.py:346
  (418 shorter events, 985.8 us)
Async XLA Ops:
  7.2 819.8 %all-gather.8.cloned.1.call-start = ((), (), s32[]{:S(2)}) async-start(), calls=%async_computation.23 | async-start | bytes 1966080 | tf_op jit(solution)/shard_map/all_gather | solution.py:216
  68.7 786.5 %all-gather.6.cloned.1.call-start = ((), (), s32[]{:S(2)}) async-start(), calls=%async_computation.22 | async-start | bytes 1966080 | tf_op jit(solution)/shard_map/all_gather | solution.py:217
  69.4 923.7 %reduce-scatter.31.cloned.1.call-start = ((), (), s32[]{:S(2)}) async-start(), calls=%async_computation.24 | async-start | bytes 2359296 | tf_op jit(solution)/shard_map/reduce_scatter | solution.py:68
  870.5 140.4 %all-gather.10.cloned.1.call-start = ((), (), s32[]{:S(2)}) async-start(), calls=%async_computation.26 | async-start | bytes 1966080 | tf_op jit(solution)/shard_map/all_gather | solution.py:201
  871.1 142.6 %all-gather.12.cloned.1.call-start = ((), (), s32[]{:S(2)}) async-start(), calls=%async_computation.27 | async-start | bytes 1966080 | tf_op jit(solution)/shard_map/all_gather | solution.py:202
  871.7 144.8 %reduce-scatter.33.cloned.1.call-start = ((), (), s32[]{:S(2)}) async-start(), calls=%async_computation.25 | async-start | bytes 2359296 | tf_op jit(solution)/shard_map/reduce_scatter | solution.py:68
  1008.3 65.4 %reduce-scatter.37.cloned.1.call-start = ((), (), s32[]{:S(2)}) async-start(), calls=%async_computation.30 | async-start | bytes 2359296 | tf_op jit(solution)/shard_map/reduce_scatter | solution.py:68
  1094.8 69.9 %reduce-scatter.69.cloned.1.call-start = ((), (), s32[]{:S(2)}) async-start(), calls=%async_computation.46 | async-start | bytes 491520
  1106.4 92.5 %reduce-scatter.43.cloned.1.call-start = ((), (), s32[]{:S(2)}) async-start(), calls=%async_computation.33 | async-start | bytes 1966080 | tf_op jit(solution)/shard_map/reduce_scatter | solution.py:76
  1131.6 99.9 %reduce-scatter.41.cloned.1.call-start = ((), (), s32[]{:S(2)}) async-start(), calls=%async_computation.32 | async-start | bytes 1966080 | tf_op jit(solution)/shard_map/reduce_scatter | solution.py:73
  1164.6 90.0 %reduce-scatter.73.cloned.1.call-start = ((), (), s32[]{:S(2)}) async-start(), calls=%async_computation.48 | async-start | bytes 737280
  1169.1 108.3 %reduce-scatter.71.cloned.1.call-start = ((), (), s32[]{:S(2)}) async-start(), calls=%async_computation.47 | async-start | bytes 737280
  1170.3 143.1 %reduce-scatter.65.cloned.1.call-start = ((), (), s32[]{:S(2)}) async-start(), calls=%async_computation.44 | async-start | bytes 1966080 | tf_op jit(solution)/shard_map/reduce_scatter | solution.py:329
  1173.8 176.0 %reduce-scatter.63.cloned.1.call-start = ((), (), s32[]{:S(2)}) async-start(), calls=%async_computation.43 | async-start | bytes 1966080 | tf_op jit(solution)/shard_map/reduce_scatter | solution.py:326
  1179.3 207.1 %reduce-scatter.61.cloned.1.call-start = ((), (), s32[]{:S(2)}) async-start(), calls=%async_computation.42 | async-start | bytes 1966080 | tf_op jit(solution)/shard_map/reduce_scatter | solution.py:323
  1180.1 229.6 %reduce-scatter.59.cloned.1.call-start = ((), (), s32[]{:S(2)}) async-start(), calls=%async_computation.41 | async-start | bytes 737280 | tf_op jit(solution)/shard_map/reduce_scatter | solution.py:320
  1181.9 250.6 %reduce-scatter.57.cloned.1.call-start = ((), (), s32[]{:S(2)}) async-start(), calls=%async_computation.40 | async-start | bytes 737280 | tf_op jit(solution)/shard_map/reduce_scatter | solution.py:311
  1183.5 271.9 %reduce-scatter.55.cloned.1.call-start = ((), (), s32[]{:S(2)}) async-start(), calls=%async_computation.39 | async-start | bytes 737280 | tf_op jit(solution)/shard_map/reduce_scatter | solution.py:308
  1186.1 292.7 %reduce-scatter.53.cloned.1.call-start = ((), (), s32[]{:S(2)}) async-start(), calls=%async_computation.38 | async-start | bytes 737280 | tf_op jit(solution)/shard_map/reduce_scatter | solution.py:302
  1235.2 266.9 %reduce-scatter.51.cloned.1.call-start = ((), (), s32[]{:S(2)}) async-start(), calls=%async_computation.37 | async-start | bytes 737280 | tf_op jit(solution)/shard_map/reduce_scatter | solution.py:296
  1235.7 289.7 %reduce-scatter.49.cloned.1.call-start = ((), (), s32[]{:S(2)}) async-start(), calls=%async_computation.36 | async-start | bytes 737280 | tf_op jit(solution)/shard_map/reduce_scatter | solution.py:293
  1236.5 1068.5 %reduce-scatter.45.cloned.1.call-start = ((), (), s32[]{:S(2)}) async-start(), calls=%async_computation.34 | async-start | bytes 2359296 | tf_op jit(solution)/shard_map/reduce_scatter | solution.py:68
  1239.0 1145.1 %all-reduce.6.cloned.1.call-start = ((), (), s32[]{:S(2)}) async-start(), calls=%async_computation.49 | async-start | bytes 4915200 | tf_op jit(solution)/shard_map/psum | solution.py:339
  1525.5 872.3 %reduce-scatter.47.cloned.1.call-start = ((), (), s32[]{:S(2)}) async-start(), calls=%async_computation.35 | async-start | bytes 589824 | tf_op jit(solution)/shard_map/reduce_scatter | solution.py:68
  (94 other events, 3190.6 us)
Sparse Core Ops, SparseCore 0:
  68.8 39.2 all-gather.7
  110.2 36.0 all-gather.5
  870.6 8.6 reduce-scatter.30
  880.7 55.6 all-gather.9
  937.8 47.0 all-gather.11
  1017.5 38.2 all-gather.13
  1090.9 10.2 reduce-scatter.38
  1103.2 10.1 reduce-scatter.34
  1115.8 22.0 reduce-scatter.68
  1140.0 18.9 reduce-scatter.66
  1161.3 33.7 reduce-scatter.42
  1197.2 34.2 reduce-scatter.40
  1233.6 20.9 reduce-scatter.72
  1256.8 20.5 reduce-scatter.70
  1279.6 33.7 reduce-scatter.64
  1315.6 34.2 reduce-scatter.62
  1352.2 34.2 reduce-scatter.60
  1388.6 20.9 reduce-scatter.58
  1412.0 20.5 reduce-scatter.56
  1434.8 20.5 reduce-scatter.54
  1458.2 20.5 reduce-scatter.52
  1481.5 20.5 reduce-scatter.50
  1504.9 20.4 reduce-scatter.48
  1539.7 77.6 all-reduce.5
  (4 shorter events, 30.9 us)
where the time goes:
time: 2450 us; the launch traced here: 2400 us
  local copies, waits for them, and re-layouts  1510 us (62%)
  waiting for transfers between devices  356 us (15%)
  blocking collectives  293 us (12%)
  matrix products  145 us (6%)
  other arithmetic  79.3 us (3%)
    unnamed x234, local copies, waits for them, and re-layouts  1400 us
    psum x1, blocking collectives, per_device(): lax.psum((grad_self_gain, grad_cross_gain, grad_ff_gain, grad_table), ('d...  72.8 us
  transfers between devices with their start and end apart: 28, of which 15 were waited for; matrix products, arithmetic and copies ran while one was open for 70% of the time, Pallas kernels for 0%

commit v1 on v0

v1 whole, which is shorter than its diff:
```python
from functools import partial

import jax
import jax.numpy as jnp
from jax import lax
from jax.experimental import pallas as pl
from jax.experimental.pallas import tpu as pltpu
from jax.sharding import PartitionSpec as P

HS = 64
PAIR = 128
EPSILON = 1e-06
NEGATIVE = -1e30
GELU_SCALE = 0.7978845608028654
BF = jnp.bfloat16
F32 = jnp.float32


def matmul(left_side, right_side):
    return jnp.dot(left_side, right_side, preferred_element_type=F32)


def matmul_t(left_side, right_side):
    return lax.dot_general(
        left_side, right_side, (((1,), (1,)), ((), ())), preferred_element_type=F32
    )


def tokens_t(left_side, right_side):
    return lax.dot_general(
        left_side, right_side, (((0,), (0,)), ((), ())), preferred_element_type=F32
    )


def gelu_parts(gate_in):
    inner_arg = GELU_SCALE * (gate_in + 0.044715 * gate_in * gate_in * gate_in)
    tangent = jnp.tanh(inner_arg)
    gelu_value = 0.5 * gate_in * (1.0 + tangent)
    gelu_slope = 0.5 * (1.0 + tangent) + 0.5 * gate_in * (1.0 - tangent * tangent) * GELU_SCALE * (
        1.0 + 3.0 * 0.044715 * gate_in * gate_in
    )
    return (gelu_value, gelu_slope)


def norm_forward(hidden, gain_vec):
    scales = lax.rsqrt(jnp.mean(hidden * hidden, axis=1, keepdims=True) + EPSILON)
    normed = hidden * scales
    return (normed, scales, (normed * gain_vec).astype(BF))


def norm_backward(upstream, normed, scales, gain_vec):
    scaled_grad = upstream * gain_vec
    average = jnp.mean(scaled_grad * normed, axis=1, keepdims=True)
    return scales * (scaled_grad - normed * average)


def table_kernel(line_ref, out_ref):
    wide = jnp.broadcast_to(line_ref[0], out_ref.shape[1:])
    out_ref[0] = pltpu.roll(wide, 0, 1, stride=1, stride_axis=0)


def build_tables(lines):
    head_count, _, width = lines.shape
    return pl.pallas_call(
        table_kernel,
        grid=(head_count,),
        in_specs=[pl.BlockSpec((1, 1, width), lambda h: (h, 0, 0))],
        out_specs=pl.BlockSpec((1, PAIR, width), lambda h: (h, 0, 0)),
        out_shape=jax.ShapeDtypeStruct((head_count, PAIR, width), F32),
        name="bias_tables",
    )(lines)


def diagonal_sums(spread):
    row_total = spread.shape[0]
    width = spread.shape[1]
    while row_total > 1:
        half = row_total // 2
        spread = spread[:half] + pltpu.roll(spread[half:], width - half, 1)
        row_total = half
        if row_total == 8:
            break
    total = spread[0:1]
    for step in range(1, 8):
        total = total + pltpu.roll(spread, width - step, 1)[step : step + 1]
    return total


def lane_pick(first_half, second_half):
    lanes = lax.broadcasted_iota(jnp.int32, first_half.shape, 1)
    return jnp.where(lanes < HS, first_half, second_half)


def head_only(values, slot):
    lanes = lax.broadcasted_iota(jnp.int32, values.shape, 1)
    keep = (lanes < HS) if slot == 0 else (lanes >= HS)
    return jnp.where(keep, values, jnp.zeros_like(values))


def forward_kernel(*refs, tile_k, biased, origin):
    if biased:
        (start_ref, q_ref, k_ref, v_ref, table_ref, pen_ref, out_ref, lse_ref) = refs
    else:
        (start_ref, q_ref, k_ref, v_ref, out_ref, lse_ref) = refs
    row_total = q_ref.shape[0]
    queries = q_ref[...]
    masked = [head_only(queries, slot) for slot in range(2)]
    first_row = start_ref[0]
    key_blocks = start_ref[1]

    def step(block, carry):
        begin = pl.multiple_of(block * tile_k, tile_k)
        keys = k_ref[pl.ds(begin, tile_k), :]
        vals = v_ref[pl.ds(begin, tile_k), :]
        fresh = []
        for slot in range(2):
            peak, total, acc = carry[slot]
            scores = matmul_t(masked[slot], keys)
            if biased:
                pieces = []
                for group in range(row_total // PAIR):
                    at = pl.multiple_of(begin - first_row - group * PAIR + origin, PAIR)
                    pieces.append(table_ref[slot, :, pl.ds(at, tile_k)])
                scores = scores + jnp.concatenate(pieces, axis=0) + pen_ref[:, pl.ds(begin, tile_k)]
            new_peak = jnp.maximum(peak, jnp.max(scores, axis=1, keepdims=True))
            decay = jnp.exp(peak - new_peak)
            probs = jnp.exp(scores - new_peak)
            total = total * decay + jnp.sum(probs, axis=1, keepdims=True)
            acc = acc * decay + matmul(probs.astype(BF), vals)
            fresh.append((new_peak, total, acc))
        return tuple(fresh)

    begin_state = tuple(
        (
            jnp.full((row_total, 1), -1e38, F32),
            jnp.zeros((row_total, 1), F32),
            jnp.zeros((row_total, PAIR), F32),
        )
        for _ in range(2)
    )
    done = lax.fori_loop(0, key_blocks, step, begin_state)
    (peak0, total0, acc0), (peak1, total1, acc1) = done
    out_ref[...] = lane_pick(acc0 / total0, acc1 / total1).astype(BF)
    for slot, (peak, total, _) in enumerate(done):
        column = jnp.broadcast_to(peak + jnp.log(total), (row_total, PAIR))
        lse_ref[slot] = column.T[:8]


def attend_forward(queries, keys, values, scalars, tables, penalty, tile_k, origin):
    row_total, width = queries.shape
    key_total = keys.shape[0]
    pairs = width // PAIR
    biased = tables is not None
    in_specs = [
        pl.BlockSpec((row_total, PAIR), lambda p, s: (0, p)),
        pl.BlockSpec((key_total, PAIR), lambda p, s: (0, p)),
        pl.BlockSpec((key_total, PAIR), lambda p, s: (0, p)),
    ]
    operands = [queries, keys, values]
    if biased:
        in_specs.append(pl.BlockSpec((2, PAIR, tables.shape[2]), lambda p, s: (p, 0, 0)))
        in_specs.append(pl.BlockSpec((1, key_total), lambda p, s: (0, 0)))
        operands += [tables, penalty]
    return pl.pallas_call(
        partial(forward_kernel, tile_k=tile_k, biased=biased, origin=origin),
        grid_spec=pltpu.PrefetchScalarGridSpec(
            num_scalar_prefetch=1,
            grid=(pairs,),
            in_specs=in_specs,
            out_specs=[
                pl.BlockSpec((row_total, PAIR), lambda p, s: (0, p)),
                pl.BlockSpec((2, 8, row_total), lambda p, s: (p, 0, 0)),
            ],
        ),
        out_shape=[
            jax.ShapeDtypeStruct((row_total, width), BF),
            jax.ShapeDtypeStruct((2 * pairs, 8, row_total), F32),
        ],
        compiler_params=pltpu.CompilerParams(vmem_limit_bytes=48 * 1024 * 1024),
        name="self_forward" if biased else "cross_forward",
    )(scalars, *operands)


def backward_kernel(*refs, tile_k, biased, origin):
    if biased:
        (
            start_ref, q_ref, k_ref, v_ref, g_ref, c_ref, lse_ref, table_ref, pen_ref,
            dq_ref, dk_ref, dv_ref, diag_ref, spread_ref,
        ) = refs
    else:
        (start_ref, q_ref, k_ref, v_ref, g_ref, c_ref, lse_ref, dq_ref, dk_ref, dv_ref) = refs
    row_total = q_ref.shape[0]
    key_total = k_ref.shape[0]
    first_row = start_ref[0]
    key_blocks = start_ref[1]
    queries = [head_only(q_ref[...], slot) for slot in range(2)]
    grads = [head_only(g_ref[...], slot) for slot in range(2)]
    product = (g_ref[...].astype(F32) * c_ref[...].astype(F32)).T
    deltas = [
        jnp.sum(product[slot * HS : (slot + 1) * HS], axis=0, keepdims=True) for slot in range(2)
    ]
    sums = [lse_ref[slot, 0:1, :] for slot in range(2)]
    if biased:
        spread_ref[...] = jnp.zeros_like(spread_ref)

    def step(block, carry):
        begin = pl.multiple_of(block * tile_k, tile_k)
        keys = k_ref[pl.ds(begin, tile_k), :]
        vals = v_ref[pl.ds(begin, tile_k), :]
        grad_keys = jnp.zeros((tile_k, PAIR), F32)
        grad_vals = jnp.zeros((tile_k, PAIR), F32)
        fresh = []
        for slot in range(2):
            scores = matmul_t(keys, queries[slot])
            if biased:
                places = []
                pieces = []
                for group in range(tile_k // PAIR):
                    at = pl.multiple_of(first_row - begin - group * PAIR + origin, PAIR)
                    places.append(at)
                    pieces.append(table_ref[slot, :, pl.ds(at, row_total)])
                scores = scores + jnp.concatenate(pieces, axis=0) + pen_ref[pl.ds(begin, tile_k), 0:1]
            probs = jnp.exp(scores - sums[slot])
            grad_probs = matmul_t(vals, grads[slot])
            dscore = probs * (grad_probs - deltas[slot])
            if biased:
                for group, at in enumerate(places):
                    spread_ref[slot, :, pl.ds(at, row_total)] += dscore[
                        group * PAIR : (group + 1) * PAIR
                    ]
            dscore_b = dscore.astype(BF)
            grad_vals = grad_vals + matmul(probs.astype(BF), grads[slot])
            grad_keys = grad_keys + matmul(dscore_b, queries[slot])
            fresh.append(carry[slot] + tokens_t(dscore_b, keys))
        dk_ref[pl.ds(begin, tile_k), :] = grad_keys.astype(BF)
        dv_ref[pl.ds(begin, tile_k), :] = grad_vals.astype(BF)
        return tuple(fresh)

    zero = jnp.zeros((row_total, PAIR), F32)
    dq0, dq1 = lax.fori_loop(0, key_blocks, step, (zero, zero))
    dq_ref[...] = lane_pick(dq0, dq1).astype(BF)

    def clear(block, carry):
        begin = pl.multiple_of(block * tile_k, tile_k)
        dk_ref[pl.ds(begin, tile_k), :] = jnp.zeros((tile_k, PAIR), BF)
        dv_ref[pl.ds(begin, tile_k), :] = jnp.zeros((tile_k, PAIR), BF)
        return carry

    lax.fori_loop(key_blocks, key_total // tile_k, clear, 0)
    if biased:
        for slot in range(2):
            diag_ref[slot] = diagonal_sums(spread_ref[slot])


def attend_backward(
    queries, keys, values, grads, context, sums, scalars, tables, penalty, tile_k, origin
):
    row_total, width = queries.shape
    key_total = keys.shape[0]
    pairs = width // PAIR
    biased = tables is not None
    row_spec = pl.BlockSpec((row_total, PAIR), lambda p, s: (0, p))
    key_spec = pl.BlockSpec((key_total, PAIR), lambda p, s: (0, p))
    in_specs = [
        row_spec, key_spec, key_spec, row_spec, row_spec,
        pl.BlockSpec((2, 8, row_total), lambda p, s: (p, 0, 0)),
    ]
    operands = [queries, keys, values, grads, context, sums]
    out_specs = [row_spec, key_spec, key_spec]
    out_shape = [
        jax.ShapeDtypeStruct((row_total, width), BF),
        jax.ShapeDtypeStruct((key_total, width), BF),
        jax.ShapeDtypeStruct((key_total, width), BF),
    ]
    scratch = []
    if biased:
        span = tables.shape[2]
        in_specs.append(pl.BlockSpec((2, PAIR, span), lambda p, s: (p, 0, 0)))
        in_specs.append(pl.BlockSpec((key_total, 1), lambda p, s: (0, 0)))
        operands += [tables, penalty]
        out_specs.append(pl.BlockSpec((2, 1, span), lambda p, s: (p, 0, 0)))
        out_shape.append(jax.ShapeDtypeStruct((2 * pairs, 1, span), F32))
        scratch.append(pltpu.VMEM((2, PAIR, span), F32))
    return pl.pallas_call(
        partial(backward_kernel, tile_k=tile_k, biased=biased, origin=origin),
        grid_spec=pltpu.PrefetchScalarGridSpec(
            num_scalar_prefetch=1,
            grid=(pairs,),
            in_specs=in_specs,
            out_specs=out_specs,
            scratch_shapes=scratch,
        ),
        out_shape=out_shape,
        compiler_params=pltpu.CompilerParams(vmem_limit_bytes=56 * 1024 * 1024),
        name="self_backward" if biased else "cross_backward",
    )(scalars, *operands)


def swap(values):
    return lax.ppermute(values, "row", [(0, 1), (1, 0)])


def join_feats(own, other):
    lower = lax.axis_index("row") == 0
    return jnp.where(
        lower, jnp.concatenate([own, other], axis=1), jnp.concatenate([other, own], axis=1)
    )


def own_feats(values):
    half = values.shape[1] // 2
    return lax.dynamic_slice_in_dim(values, lax.axis_index("row") * half, half, axis=1)


def other_feats(values):
    half = values.shape[1] // 2
    return lax.dynamic_slice_in_dim(values, (1 - lax.axis_index("row")) * half, half, axis=1)


def gather_weights(packed):
    return lax.all_gather(packed, "col", axis=0, tiled=True)


def scatter_weights(grads):
    mine = lax.psum_scatter(grads, "col", scatter_dimension=0, tiled=True)
    return lax.psum(mine, "dp")


def per_device(
    hidden_in, enc_states, grad_out, lengths, buckets,
    self_gain, q_self, k_self, v_self, o_self, rel_table,
    cross_gain, q_cross, k_cross, v_cross, o_cross,
    ff_gain, ff_gate, ff_up, ff_out,
):
    row_total, half = hidden_in.shape
    enc_rows = enc_states.shape[0]
    seq_len = row_total * lax.axis_size("col")
    first_row = lax.axis_index("col") * row_total
    wide = q_self.shape[1]
    ff_cols = ff_gate.shape[1]
    valid = lengths[0]

    self_w = gather_weights(jnp.concatenate([q_self, k_self, v_self], axis=1))
    rest_w = gather_weights(
        jnp.concatenate([o_self.T, q_cross, o_cross.T, k_cross, v_cross], axis=1)
    )
    ff_w = gather_weights(jnp.concatenate([ff_gate, ff_up, ff_out.T], axis=1))
    w_qkv = self_w
    o_self_t = rest_w[:, :wide]
    w_cq = rest_w[:, wide : 2 * wide]
    o_cross_t = rest_w[:, 2 * wide : 3 * wide]
    w_ckv = rest_w[:, 3 * wide :]
    w_gu = ff_w[:, : 2 * ff_cols]
    ff_out_t = ff_w[:, 2 * ff_cols :]

    packed_in = jnp.concatenate([hidden_in, enc_states, grad_out], axis=0)
    whole_in = join_feats(packed_in, swap(packed_in))
    residual = whole_in[:row_total].astype(F32)
    enc_whole = whole_in[row_total : row_total + enc_rows]
    upstream_b = whole_in[row_total + enc_rows :]
    gains = jnp.stack([self_gain, cross_gain, ff_gain])
    gains = join_feats(gains, swap(gains))
    gain1, gain2, gain3 = gains[0:1], gains[1:2], gains[2:3]

    tile_f = min(512, row_total)
    tile_b = min(256, row_total)
    reach = max(row_total, tile_f)
    onehot = (buckets[:, None] == jnp.arange(rel_table.shape[1])[None, :]).astype(F32)
    bias_dist = jnp.dot(rel_table, onehot.T, precision=lax.Precision.HIGHEST)
    head_count = bias_dist.shape[0]
    back_dist = jnp.flip(bias_dist, axis=1)
    origin_f = seq_len - PAIR
    origin_b = max(row_total, tile_b) - PAIR
    never = lambda count: jnp.full((head_count, count), NEGATIVE, F32)
    line_f = jnp.concatenate(
        [back_dist[:, PAIR - 1 :], never(reach), back_dist[:, : PAIR - 1]], axis=1
    )
    pad_f = (-line_f.shape[1]) % PAIR
    line_f = jnp.concatenate(
        [back_dist[:, PAIR - 1 :], never(reach + pad_f), back_dist[:, : PAIR - 1]], axis=1
    )
    line_b = jnp.concatenate([never(origin_b), bias_dist, never(PAIR)], axis=1)
    tables_f = build_tables(line_f[:, None, :])
    tables_b = build_tables(line_b[:, None, :])
    penalty = jnp.where(jnp.arange(seq_len) < valid, 0.0, NEGATIVE).astype(F32)
    last_key = jnp.minimum(first_row + row_total, valid)
    scalars_f = jnp.stack([first_row, (last_key + tile_f - 1) // tile_f]).astype(jnp.int32)
    scalars_b = jnp.stack([first_row, (last_key + tile_b - 1) // tile_b]).astype(jnp.int32)

    normed1, scales1, input1 = norm_forward(residual, gain1)
    qkv = matmul(input1, w_qkv).astype(BF)
    kv_all = lax.all_gather(qkv[:, wide:], "col", axis=0, tiled=True)
    keys_s, vals_s = kv_all[:, :wide], kv_all[:, wide:]
    cross_own = matmul(enc_whole, w_ckv).astype(BF)
    ckv_all = lax.all_gather(cross_own, "col", axis=0, tiled=True)
    keys_c, vals_c = ckv_all[:, :wide], ckv_all[:, wide:]
    queries_s = qkv[:, :wide]
    context, sums_s = attend_forward(
        queries_s, keys_s, vals_s, scalars_f, tables_f, penalty[None, :], tile_f, origin_f
    )
    part = matmul_t(context, o_self_t)
    after_self = residual + (part + swap(part))

    normed2, scales2, input2 = norm_forward(after_self, gain2)
    queries_c = matmul(input2, w_cq).astype(BF)
    tile_cf = min(512, keys_c.shape[0])
    tile_cb = min(256, keys_c.shape[0])
    scalars_cf = jnp.array([0, keys_c.shape[0] // tile_cf], jnp.int32)
    scalars_cb = jnp.array([0, keys_c.shape[0] // tile_cb], jnp.int32)
    context_c, sums_c = attend_forward(
        queries_c, keys_c, vals_c, scalars_cf, None, None, tile_cf, 0
    )
    part = matmul_t(context_c, o_cross_t)
    after_cross = after_self + (part + swap(part))

    normed3, scales3, input3 = norm_forward(after_cross, gain3)
    gate_up = matmul(input3, w_gu)
    gate_part = gate_up[:, :ff_cols]
    up_part = gate_up[:, ff_cols:]
    activated, gelu_slope = gelu_parts(gate_part)
    hidden_units = (activated * up_part).astype(BF)
    grad_hidden = matmul(upstream_b, ff_out_t)
    grad_gate_up = jnp.concatenate(
        [grad_hidden * up_part * gelu_slope, grad_hidden * activated], axis=1
    ).astype(BF)
    part3 = matmul_t(grad_gate_up, w_gu)
    grad_input3 = part3 + swap(part3)
    part = matmul_t(hidden_units, ff_out_t)
    output = (own_feats(after_cross) + (own_feats(part) + swap(other_feats(part)))).astype(BF)
    grad_ff = jnp.concatenate(
        [tokens_t(input3, grad_gate_up).astype(BF), tokens_t(upstream_b, hidden_units).astype(BF)],
        axis=1,
    )
    sum_ff = scatter_weights(grad_ff)
    grad_ff_gain = own_feats(jnp.sum(grad_input3 * normed3, axis=0, keepdims=True))
    grad_after_cross = upstream_b.astype(F32) + norm_backward(
        grad_input3, normed3, scales3, gain3
    )

    down_cross = grad_after_cross.astype(BF)
    grad_context_c = matmul(down_cross, o_cross_t).astype(BF)
    grad_cq, grad_ck, grad_cv = attend_backward(
        queries_c, keys_c, vals_c, grad_context_c, context_c, sums_c,
        scalars_cb, None, None, tile_cb, 0,
    )
    grad_ckv = lax.psum_scatter(
        jnp.concatenate([grad_ck, grad_cv], axis=1), "col", scatter_dimension=0, tiled=True
    )
    part = matmul_t(grad_cq, w_cq)
    grad_input2 = part + swap(part)
    grad_cross_gain = own_feats(jnp.sum(grad_input2 * normed2, axis=0, keepdims=True))
    grad_after_self = grad_after_cross + norm_backward(grad_input2, normed2, scales2, gain2)
    part = matmul_t(grad_ckv, w_ckv)
    grad_encoder = own_feats(part) + swap(other_feats(part))

    down_self = grad_after_self.astype(BF)
    grad_context = matmul(down_self, o_self_t).astype(BF)
    grad_q, grad_k, grad_v, diag = attend_backward(
        queries_s, keys_s, vals_s, grad_context, context, sums_s,
        scalars_b, tables_b, penalty[:, None], tile_b, origin_b,
    )
    grad_kv = lax.psum_scatter(
        jnp.concatenate([grad_k, grad_v], axis=1), "col", scatter_dimension=0, tiled=True
    )
    grad_rest = jnp.concatenate(
        [
            tokens_t(down_self, context).astype(BF),
            tokens_t(input2, grad_cq).astype(BF),
            tokens_t(down_cross, context_c).astype(BF),
            tokens_t(enc_whole, grad_ckv).astype(BF),
        ],
        axis=1,
    )
    sum_rest = scatter_weights(grad_rest)
    grad_dist = diag[:, 0, origin_b : origin_b + seq_len]
    grad_table = jnp.dot(grad_dist, onehot, precision=lax.Precision.HIGHEST)
    grad_qkv = jnp.concatenate([grad_q, grad_kv], axis=1)
    part = matmul_t(grad_qkv, w_qkv)
    grad_input1 = part + swap(part)
    sum_qkv = scatter_weights(tokens_t(input1, grad_qkv).astype(BF))
    grad_self_gain = own_feats(jnp.sum(grad_input1 * normed1, axis=0, keepdims=True))
    grad_input = own_feats(
        grad_after_self + norm_backward(grad_input1, normed1, scales1, gain1)
    )
    small = lax.psum(
        (grad_self_gain[0], grad_cross_gain[0], grad_ff_gain[0], grad_table), ("dp", "col")
    )
    sum_qkv = sum_qkv.astype(F32)
    sum_rest = sum_rest.astype(F32)
    sum_ff = sum_ff.astype(F32)
    return (
        output,
        grad_input,
        grad_encoder,
        small[0],
        sum_qkv[:, :wide],
        sum_qkv[:, wide : 2 * wide],
        sum_qkv[:, 2 * wide :],
        sum_rest[:, :wide].T,
        small[3],
        small[1],
        sum_rest[:, wide : 2 * wide],
        sum_rest[:, 3 * wide : 4 * wide],
        sum_rest[:, 4 * wide :],
        sum_rest[:, 2 * wide : 3 * wide].T,
        small[2],
        sum_ff[:, :ff_cols],
        sum_ff[:, ff_cols : 2 * ff_cols],
        sum_ff[:, 2 * ff_cols :].T,
    )


def solution(mesh):
    tokens = P(("dp", "col"), "row")
    stored = P("col", "row")
    turned = P("row", "col")
    return jax.shard_map(
        per_device,
        mesh=mesh,
        in_specs=(
            tokens, tokens, tokens, P("dp"), P(),
            P("row"), stored, stored, stored, turned, P("row", None),
            P("row"), stored, stored, stored, turned,
            P("row"), stored, stored, turned,
        ),
        out_specs=(
            tokens, tokens, tokens,
            P("row"), stored, stored, stored, turned, P("row", None),
            P("row"), stored, stored, stored, turned,
            P("row"), stored, stored, turned,
        ),
        check_vma=False,
    )
```

time: 2450 us -> 730 us (0.30); the launches traced: 2400 us -> 729 us
  local copies, waits for them, and re-layouts: 1510 us -> 41.7 us
  blocking collectives: 293 us -> 102 us
  matrix products: 145 us -> 48.8 us
  waiting for transfers between devices: 356 us -> 427 us
  Pallas kernels: 0 us -> 53.6 us
  other arithmetic: 79.3 us -> 37.3 us
    unnamed x234 -> x138, local copies, waits for them, and re-layouts: 1400 us -> 25.3 us
    all_gather x17 -> x1, blocking collectives: 206 us -> 26.9 us  [per_device(): ckv_all = lax.all_gather(cross_own, 'col', axis=0, tiled=True)]
    all_gather x5 -> x4, waiting for transfers between devices: 26.3 us -> 189 us  [the longest x3 142 us: gather_weights(): return lax.all_gather(packed, 'col', axis=0, tiled=True)]
    reduce_scatter x18 -> x4, waiting for transfers between devices: 289 us -> 185 us  [the longest x2 127 us: scatter_weights(): mine = lax.psum_scatter(grads, 'col', scatter_dimension=0, tiled=True)]
    dot_general x21 -> x9, matrix products: 115 us -> 19.5 us  [the longest x7 18 us: matmul(): return jnp.dot(left_side, right_side, preferred_element_type=F32)]
    pallas_call x0 -> x6, Pallas kernels: none -> 53.6 us  [the longest x2 27 us: attend_backward(): pl.pallas_call(partial(backward_kernel, tile_k=tile_k, biased=biased, ori...]
    pad x2 -> x0, local copies, waits for them, and re-layouts: 48.6 us -> none  [the longest x1 27.9 us: toeplitz(): tiled_rows[:, :row_total * (span_width - 1)]]
    reshape x1 -> x0, local copies, waits for them, and re-layouts: 44.5 us -> none  [toeplitz(): tiled_rows[:, :row_total * (span_width - 1)]]
  transfers between devices with their start and end apart: 28 -> 19, of which waited for: 15 -> 12; matrix products, arithmetic and copies ran while one was open for 70% -> 12% of each run, Pallas kernels for 0% -> 6%
where the time goes in v1:
time: 730 us; the launch traced here: 729 us
  waiting for transfers between devices  427 us (58%)
  blocking collectives  102 us (14%)
  Pallas kernels  53.6 us (7%)
  matrix products  48.8 us (7%)
  local copies, waits for them, and re-layouts  41.7 us (6%)
  other arithmetic  37.3 us (5%)
  between operations  15.8 us (2%)
    all_gather x3, waiting for transfers between devices, gather_weights(): return lax.all_gather(packed, 'col', axis=0, tiled=True)  142 us
    reduce_scatter x2, waiting for transfers between devices, scatter_weights(): mine = lax.psum_scatter(grads, 'col', scatter_dimension=0, tiled=True)  127 us
    psum x1, blocking collectives, per_device(): lax.psum((grad_self_gain[0], grad_cross_gain[0], grad_ff_gain[0], grad_ta...  75.1 us
    reduce_scatter x1, waiting for transfers between devices, per_device(): lax.psum_scatter(jnp.concatenate([grad_k, grad_v], axis=1), 'col', scatte...  58.1 us
    all_gather x1, waiting for transfers between devices, per_device(): kv_all = lax.all_gather(qkv[:, wide:], 'col', axis=0, tiled=True)  47.3 us
    unnamed x11, waiting for transfers between devices  45 us
    pallas_call x2, Pallas kernels, attend_backward(): pl.pallas_call(partial(backward_kernel, tile_k=tile_k, biased=biased, ori...  27 us
    all_gather x1, blocking collectives, per_device(): ckv_all = lax.all_gather(cross_own, 'col', axis=0, tiled=True)  26.9 us
  transfers between devices with their start and end apart: 19, of which 12 were waited for; matrix products, arithmetic and copies ran while one was open for 12% of the time, Pallas kernels for 6%

profile of v1, /device:TPU:0, one launch (start us, length us, event | category | flops | bytes accessed | tf_op | source)
XLA Modules:
  0.0 728.7 jit_solution(6370677811731718195)
XLA Ops:
  13.5 39.8 %all-gather.5.cloned.1.call-done = bf16[768,1152]{1,0:T(8,128)(2,1)} async-done(((bf16[192,1152]{1,0:T(8,128)(2,1)}), bf16[768,1152]{1,0:T(8,128)(2,1)}) %all-gather.5.cloned.1.call-update) | async-done | bytes 1769488 | tf_op jit(solution)/shard_map/all_gather | solution.py:321
  66.0 6.0 bias_tables.2.refs_4_
  72.1 47.3 %all-gather.7.cloned.1.call-done = bf16[2048,768]{1,0:T(8,128)(2,1)} async-done(((bf16[512,768]{1,0:T(8,128)(2,1)}), bf16[2048,768]{1,0:T(8,128)(2,1)}) %all-gather.7.cloned.1.call-update) | async-done | bytes 3145744 | tf_op jit(solution)/shard_map/all_gather | solution.py:392
  121.6 8.6 %self_forward.1 = (bf16[512,384]{1,0:T(8,128)(2,1)S(1)}, f32[6,8,512]{2,1,0:T(8,128)S(1)}) custom-call(s32[2]{0:T(128)S(1)} %pad_add_fusion.refs_0_, bf16[512,384]{1,0:T(8,128)(2,1)S(1)} %slice.146.refs_1_, bf16[2048,384]{1,0:T(8,128)(2,1)S(1)} %get-tuple-element.101.refs_2_, bf16[2048,384]{1,0:T(8,128)(2,1)S(1)} %get-tuple-element.100.refs_3_, ...), custom_call_target="tpu_custom_call" | custom-call | tf_op jit(solution)/shard_map/self_forward/pallas_call | solution.py:164
  131.7 48.7 %all-gather.9.cloned.1.call-done = bf16[768,1920]{1,0:T(8,128)(2,1)} async-done(((bf16[192,1920]{1,0:T(8,128)(2,1)}), bf16[768,1920]{1,0:T(8,128)(2,1)}) %all-gather.9.cloned.1.call-update) | async-done | bytes 2949136 | tf_op jit(solution)/shard_map/all_gather | solution.py:321
  184.0 26.9 %all_gather.18 = bf16[512,768]{1,0:T(8,128)(2,1)S(1)} all-gather(bf16[128,768]{1,0:T(8,128)(2,1)S(1)} %convolution_convert_fusion.11), channel_id=1, replica_groups=mesh['dp'=4,'row'=2,'col'=4] {'col'}, dimensions={0}, use_global_device_ids=true | all-gather | bytes 983040 | tf_op jit(solution)/shard_map/all_gather | solution.py:395
  213.1 6.1 cross_forward.1
  221.2 3.4 collective-permute-done.3
  224.9 53.1 %all-gather.11.cloned.1.call-done = bf16[768,3072]{1,0:T(8,128)(2,1)} async-done(((bf16[192,3072]{1,0:T(8,128)(2,1)}), bf16[768,3072]{1,0:T(8,128)(2,1)}) %all-gather.11.cloned.1.call-update) | async-done | bytes 4718608 | tf_op jit(solution)/shard_map/all_gather | solution.py:321
  278.0 3.9 fusion.2
  281.9 3.3 fusion.10
  296.2 10.1 %cross_backward.1 = (bf16[512,384]{1,0:T(8,128)(2,1)}, bf16[512,384]{1,0:T(8,128)(2,1)}, bf16[512,384]{1,0:T(8,128)(2,1)}) custom-call(s32[2]{0:T(128)} %iota_multiply_fusion.refs_0_, bf16[512,384]{1,0:T(8,128)(2,1)} %copy-done.9, bf16[512,384]{1,0:T(8,128)(2,1)} %copy-done.8, bf16[512,384]{1,0:T(8,128)(2,1)} %copy-done.7, ...), custom_call_target="tpu_custom_call" | custom-call | tf_op jit(solution)/shard_map/cross_backward/pallas_call | solution.py:284
  317.7 6.0 bias_tables.3.refs_7_
  332.8 16.8 %self_backward.1 = (bf16[512,384]{1,0:T(8,128)(2,1)}, bf16[2048,384]{1,0:T(8,128)(2,1)}, bf16[2048,384]{1,0:T(8,128)(2,1)}, f32[6,1,2560]{2,1,0:T(1,128)}) custom-call(s32[2]{0:T(128)} %pad_add_fusion.1.refs_0_, bf16[512,384]{1,0:T(8,128)(2,1)} %copy-done.6, bf16[2048,384]{1,0:T(8,128)(2,1)} %copy-done.3, bf16[2048,384]{1,0:T(8,128)(2,1)} %copy-done.2, ...), custom_call_target="tpu_custom_call" | custom-call | tf_op jit(solution)/shard_map/self_backward/pallas_call | solution.py:284
  349.6 3.8 pad_maximum_fusion.1
  361.8 4.6 copy.52
  375.5 58.1 %reduce-scatter.8.cloned.1.call-done = bf16[512,768]{1,0:T(8,128)(2,1)} async-done(((bf16[2048,768]{1,0:T(8,128)(2,1)}), bf16[512,768]{1,0:T(8,128)(2,1)}) %reduce-scatter.8.cloned.1.call-update) | async-done | bytes 786448 | tf_op jit(solution)/shard_map/reduce_scatter | solution.py:462
  435.7 4.0 convolution_convert_fusion.1
  440.1 3.1 fusion.14
  448.3 44.9 %reduce-scatter.16.cloned.1.call-done = bf16[192,1920]{1,0:T(8,128)(2,1)} async-done(((bf16[768,1920]{1,0:T(8,128)(2,1)}), bf16[192,1920]{1,0:T(8,128)(2,1)}) %reduce-scatter.16.cloned.1.call-update) | async-done | bytes 737296
  495.4 85.2 %reduce-scatter.14.cloned.1.call-done = bf16[192,3072]{1,0:T(8,128)(2,1)} async-done(((bf16[768,3072]{1,0:T(8,128)(2,1)}), bf16[192,3072]{1,0:T(8,128)(2,1)}) %reduce-scatter.14.cloned.1.call-update) | async-done | bytes 1179664 | tf_op jit(solution)/shard_map/reduce_scatter | solution.py:325
  580.5 41.4 %reduce-scatter.12.cloned.1.call-done = bf16[192,1152]{1,0:T(8,128)(2,1)} async-done(((bf16[768,1152]{1,0:T(8,128)(2,1)}), bf16[192,1152]{1,0:T(8,128)(2,1)}) %reduce-scatter.12.cloned.1.call-update) | async-done | bytes 442384 | tf_op jit(solution)/shard_map/reduce_scatter | solution.py:325
  628.5 4.7 multiply_reduce_fusion.2
  633.2 75.1 %all-reduce = (f32[384]{0:T(512)}, f32[6,32]{1,0:T(8,128)}, f32[384]{0:T(512)}, f32[384]{0:T(512)}) all-reduce(f32[384]{0:T(512)S(1)} %squeeze.16, f32[6,32]{1,0:T(8,128)S(1)} %fusion.16, f32[384]{0:T(512)S(1)} %squeeze.18, f32[384]{0:T(512)S(1)} %squeeze.19), channel_id=1, replica_groups=mesh['dp'=4,'row'=2,'col'=4] {'dp','col'}, use_global_device_ids=true, to_apply=%region_9.10 | all-reduce | flops 1344 | bytes 10752 | tf_op jit(solution)/shard_map/psum | solution.py:485
  (259 shorter events, 108.1 us)
Async XLA Ops:
  7.2 55.7 %copy-start = (f32[6,32]{1,0:T(8,128)S(1)}, f32[6,32]{1,0:T(8,128)}, u32[]{:S(2)}) copy-start(f32[6,32]{1,0:T(8,128)} %param.32) | copy-start | bytes 2308
  7.3 46.0 %all-gather.5.cloned.1.call-start = ((), (), s32[]{:S(2)}) async-start(), calls=%async_computation.5 | async-start | bytes 2211840 | tf_op jit(solution)/shard_map/all_gather | solution.py:321
  9.3 110.1 %all-gather.7.cloned.1.call-start = ((), (), s32[]{:S(2)}) async-start(), calls=%async_computation.6 | async-start | bytes 3932160 | tf_op jit(solution)/shard_map/all_gather | solution.py:392
  9.5 3.2 collective-permute-start
  10.1 2.0 collective-permute-start.1
  57.0 123.4 %all-gather.9.cloned.1.call-start = ((), (), s32[]{:S(2)}) async-start(), calls=%async_computation.7 | async-start | bytes 3686400 | tf_op jit(solution)/shard_map/all_gather | solution.py:321
  60.9 217.1 %all-gather.11.cloned.1.call-start = ((), (), s32[]{:S(2)}) async-start(), calls=%async_computation.8 | async-start | bytes 5898240 | tf_op jit(solution)/shard_map/all_gather | solution.py:321
  62.2 295.0 %reduce-scatter.10.cloned.1.call-start = ((), (), s32[]{:S(2)}) async-start(), calls=%async_computation.10 | async-start | bytes 983040 | tf_op jit(solution)/shard_map/reduce_scatter | solution.py:446
  182.3 28.7 %collective-permute-start.2 = (f32[512,768]{1,0:T(8,128)S(1)}, f32[512,768]{1,0:T(8,128)S(1)}, u32[]{:S(2)}, u32[]{:S(2)}) collective-permute-start(f32[512,768]{1,0:T(8,128)S(1)} %fusion.33), channel_id=1, source_target_pairs={{0,4},{4,0},{1,5},{5,1},{2,6},{6,2},{3,7},{7,3},{8,12},{12,8},{9,1... | collective-permute-start | bytes 4718600 | tf_op jit(solution)/shard_map/ppermute | solution.py:300
  221.1 56.9 %copy-start.43 = (f32[768]{0:T(1024)S(1)}, f32[768]{0:T(1024)}, u32[]{:S(2)}) copy-start(f32[768]{0:T(1024)} %get-tuple-element.82) | copy-start | bytes 9220
  221.1 3.5 collective-permute-start.3
  224.9 65.7 %copy-start.16 = (f32[512,768]{1,0:T(8,128)}, f32[512,768]{1,0:T(8,128)S(1)}, u32[]{:S(2)}) copy-start(f32[512,768]{1,0:T(8,128)S(1)} %get-tuple-element.94) | copy-start | bytes 4718596
  287.1 3.5 collective-permute-start.5
  309.4 14.3 %collective-permute-start.6 = (f32[512,768]{1,0:T(8,128)}, f32[512,768]{1,0:T(8,128)}, u32[]{:S(2)}, u32[]{:S(2)}) collective-permute-start(f32[512,768]{1,0:T(8,128)} %fusion.29), channel_id=1, source_target_pairs={{0,4},{4,0},{1,5},{5,1},{2,6},{6,2},{3,7},{7,3},{8,12},{12,8},{9,1... | collective-permute-start | bytes 4718600 | tf_op jit(solution)/shard_map/ppermute | solution.py:300
  315.3 118.3 %reduce-scatter.8.cloned.1.call-start = ((), (), s32[]{:S(2)}) async-start(), calls=%async_computation.9 | async-start | bytes 3932160 | tf_op jit(solution)/shard_map/reduce_scatter | solution.py:462
  353.4 139.7 %reduce-scatter.16.cloned.1.call-start = ((), (), s32[]{:S(2)}) async-start(), calls=%async_computation.13 | async-start | bytes 3686400
  366.4 214.1 %reduce-scatter.14.cloned.1.call-start = ((), (), s32[]{:S(2)}) async-start(), calls=%async_computation.12 | async-start | bytes 5898240 | tf_op jit(solution)/shard_map/reduce_scatter | solution.py:325
  373.7 62.0 %copy-start.45 = (f32[512]{0:T(512)S(1)}, f32[512]{0:T(512)}, u32[]{:S(2)}) copy-start(f32[512]{0:T(512)} %copy-done.44) | copy-start | bytes 6148
  373.7 62.0 %copy-start.47 = (f32[768]{0:T(1024)S(1)}, f32[768]{0:T(1024)}, u32[]{:S(2)}) copy-start(f32[768]{0:T(1024)} %copy-done.46) | copy-start | bytes 9220
  373.7 248.2 %reduce-scatter.12.cloned.1.call-start = ((), (), s32[]{:S(2)}) async-start(), calls=%async_computation.11 | async-start | bytes 2211840 | tf_op jit(solution)/shard_map/reduce_scatter | solution.py:325
  439.8 270.8 %all-reduce.4.cloned.1.call-start = ((), (), s32[]{:S(2)}) async-start(), calls=%async_computation.14 | async-start | bytes 5210112 | tf_op jit(solution)/shard_map/psum | solution.py:326
  445.3 176.7 %collective-permute-start.4 = (f32[512,384]{1,0:T(8,128)}, f32[512,384]{1,0:T(8,128)}, u32[]{:S(2)}, u32[]{:S(2)}) collective-permute-start(f32[512,384]{1,0:T(8,128)} %constant_dynamic-slice_fusion.1), channel_id=1, source_target_pairs={{0,4},{4,0},{1,5},{5,1},{2,6},{6,2},{3,7},{7,3},{8,12},{12,8},{9,1... | collective-permute-start | bytes 2359304 | tf_op jit(solution)/shard_map/ppermute | solution.py:300
  448.3 180.2 %collective-permute-start.7 = (f32[512,768]{1,0:T(8,128)}, f32[512,768]{1,0:T(8,128)}, u32[]{:S(2)}, u32[]{:S(2)}) collective-permute-start(f32[512,768]{1,0:T(8,128)} %fusion.50), channel_id=1, source_target_pairs={{0,4},{4,0},{1,5},{5,1},{2,6},{6,2},{3,7},{7,3},{8,12},{12,8},{9,1... | collective-permute-start | bytes 4718600 | tf_op jit(solution)/shard_map/ppermute | solution.py:300
  626.3 1.5 collective-permute-start.8
  (56 other events, 319.9 us)
Sparse Core Ops, SparseCore 0:
  10.2 42.9 all-gather.4
  57.1 62.2 all-gather.6
  121.6 58.8 all-gather.8
  181.8 96.1 all-gather.10
  315.4 22.3 reduce-scatter.9
  353.6 79.9 reduce-scatter.7
  435.9 57.2 reduce-scatter.15
  495.5 85.0 reduce-scatter.13
  582.9 39.0 reduce-scatter.11
  625.2 77.8 all-reduce.3
